TPU v7x, 32 devices: a whole 2x2x4 slice. The times are simulated.
32 devices in a mesh: groups: 2 (over x), branch: 2 (over core), sub: 8 (over z, y).
Axes of the slice: x: 2, y: 2, z: 4, core: 2. Of those that a mesh axis runs over, the one named last changes fastest.
Arguments:
- dispatch: float32 [128, 168, 2048], P(('groups', 'branch', 'sub')), parts along dimension 0, may hold values from 0 to 3
- multiplier: float32 [128, 48, 2048], P(('groups', 'branch', 'sub')), parts along dimension 0, may hold values from -3 to 3
- node_of: int32 [128], P(('groups', 'branch', 'sub')), parts along dimension 0, may hold values from 0 to 7, as said below
- prob_weight: int32 [128], P(('groups', 'branch', 'sub')), parts along dimension 0, may hold values from 1 to 16
- commitment: int32 [128, 168, 2048], P(('groups', 'branch', 'sub')), parts along dimension 0, may hold values 0 or 1
- zone_of: int32 [2048], replicated, may hold values from 0 to 31
- capacity: float32 [2048], replicated, may hold values from 0.5 to 4
- linear_cost: float32 [2048], replicated, may hold values from -0.5 to 1
- quad_cost: float32 [2048], replicated, may hold values from 0.5 to 2
- demand: float32 [128, 168, 32], P(('groups', 'branch', 'sub')), parts along dimension 0, may hold values from 19 to 64
Outputs:
- new_dispatch: float32 [128, 168, 2048], P(('groups', 'branch', 'sub')), parts along dimension 0
- new_multiplier: float32 [128, 48, 2048], P(('groups', 'branch', 'sub')), parts along dimension 0
- next_average: float32 [128, 48, 2048], P(('groups', 'branch', 'sub')), parts along dimension 0
- deviation: float32 [2], P('groups'), parts along dimension 0
There are 2 independent parts, one for each index of `groups`. A program takes and returns all parts, laid end to end along the dimension named above; an argument that names none is the same for every part. Nothing has to cross between parts.
Inputs may be any that keep to these rules, and one draw needn't show every extreme that they name: `node_of`: within each aligned block of 32 scenarios (one day-one branch), every node number holds exactly 4 scenarios.
All inputs are finite; a program needn't handle non-finite values. No bound on the sum of `commitment` on one device may be relied on, other than what follows from the above.
Results may differ from a plain program's by a relative error of at most 0.0001.
Values sent between devices are 32-bit elements; how exact they have to be, the bound alone decides.
A program may use at most 128 MiB of HBM per device.

v0:
```python
import jax
import jax.numpy as jnp
from jax import lax
from jax.sharding import PartitionSpec as P

DAY = 24
NODES_BR = 8
STEPS = 3


rho_value = 1.0
step_size = 0.3


def average(early_part, prob_weight, node_of, riding):
    weighting = prob_weight.astype(jnp.float32)
    scen_local = early_part.shape[0]
    gens = early_part.shape[2]
    member = (node_of[None, :] == jnp.arange(NODES_BR, dtype=jnp.int32)[:, None]).astype(
        jnp.float32
    )
    weighted = member * weighting[None, :]
    day_one = jnp.einsum(
        "s,stg->tg", weighting, early_part[:, :DAY], precision=lax.Precision.HIGHEST
    )
    weight_sum = jnp.sum(weighting)[None]
    day_two = jnp.einsum(
        "ks,stg->ktg", weighted, early_part[:, DAY:], precision=lax.Precision.HIGHEST
    )
    node_weight = jnp.sum(weighted, axis=1)
    day_two, node_weight = lax.psum((day_two, node_weight), "sub")
    day_one, weight_sum, riding = lax.psum((day_one, weight_sum, riding), ("branch", "sub"))
    root_mean = day_one / weight_sum[0]
    node_mean = day_two / node_weight[:, None, None]
    assigned = jnp.einsum("ks,ktg->stg", member, node_mean, precision=lax.Precision.HIGHEST)
    spread_root = jnp.broadcast_to(root_mean[None], (scen_local, DAY, gens))
    return (jnp.concatenate([spread_root, assigned], axis=1), weight_sum, riding)


def shards(
    dispatch,
    multiplier,
    node_of,
    prob_weight,
    commitment,
    zone_of,
    capacity,
    linear_cost,
    quad_cost,
    demand,
):
    section_hours = multiplier.shape[1]
    gens = zone_of.shape[0]
    zones_count = demand.shape[2]
    weighting = prob_weight.astype(jnp.float32)
    nothing = jnp.zeros((1,), jnp.float32)
    averages, weight_sum, unused = average(
        dispatch[:, :section_hours], prob_weight, node_of, nothing
    )
    spread_gap = dispatch[:, :section_hours] - averages
    local_spread = jnp.sum(weighting[:, None, None] * spread_gap * spread_gap)[None]
    dev_total = lax.psum(local_spread, ("branch", "sub"))
    new_multiplier = multiplier + rho_value * spread_gap
    zone_table = (zone_of[:, None] == jnp.arange(zones_count, dtype=jnp.int32)[None, :]).astype(
        jnp.float32
    )
    ceiling = capacity[None, None, :] * commitment.astype(jnp.float32)
    balance = zones_count / gens
    current = dispatch
    for sweep in range(STEPS):
        zone_sum = jnp.einsum("stg,gz->stz", current, zone_table, precision=lax.Precision.HIGHEST)
        mismatch = zone_sum - demand
        feedback = jnp.einsum("stz,gz->stg", mismatch, zone_table, precision=lax.Precision.HIGHEST)
        gradient = linear_cost + quad_cost * current + balance * feedback
        hedged = (
            gradient[:, :section_hours]
            + new_multiplier
            + rho_value * (current[:, :section_hours] - averages)
        )
        gradient = jnp.concatenate([hedged, gradient[:, section_hours:]], axis=1)
        current = jnp.clip(current - step_size * gradient, 0.0, ceiling)
    next_average, unused_sum, carried = average(
        current[:, :section_hours], prob_weight, node_of, nothing
    )
    deviation = dev_total / (weight_sum * section_hours * gens)
    return (current, new_multiplier, next_average, deviation)


def solution(mesh):
    in_specs = (
        P(("groups", "branch", "sub"), None, None),
        P(("groups", "branch", "sub"), None, None),
        P(("groups", "branch", "sub")),
        P(("groups", "branch", "sub")),
        P(("groups", "branch", "sub"), None, None),
        P(),
        P(),
        P(),
        P(),
        P(("groups", "branch", "sub"), None, None),
    )
    out_specs = (
        P(("groups", "branch", "sub"), None, None),
        P(("groups", "branch", "sub"), None, None),
        P(("groups", "branch", "sub"), None, None),
        P("groups"),
    )
    return jax.shard_map(shards, mesh=mesh, in_specs=in_specs, out_specs=out_specs, check_vma=False)
```

profile of v0, /device:TPU:0, one launch (start us, length us, event | category | flops | bytes accessed | tf_op | source)
XLA Modules:
  0.0 428.4 jit_solution(12756518674870253161)
XLA Ops:
  7.3 1.5 fusion.62
  8.8 2.5 fusion.25
  11.3 0.7 copy.33
  12.0 0.0 all-reduce.7.cloned.1.call-start
  12.1 0.7 convert_element_type.5
  12.7 4.0 fusion.23
  16.8 0.6 convert_reduce_fusion
  17.4 0.1 select_reduce_fusion
  17.5 35.9 %psum.56 = f32[1]{0:T(128)} all-reduce(f32[1]{0:T(128)} %bitcast.4), channel_id=1, replica_groups=mesh['groups'=2,'branch'=2,'sub'=8] {'branch','sub'}, use_global_device_ids=true, to_apply=%region_2.0 | all-reduce | flops 1 | bytes 8 | tf_op jit(solution)/shard_map/psum | solution.py:32
  53.4 17.6 %psum.58 = f32[8]{0:T(128)S(1)} all-reduce(f32[8]{0:T(128)S(1)} %select_reduce_fusion), channel_id=1, replica_groups=mesh['groups'=2,'branch'=2,'sub'=8] {'sub'}, use_global_device_ids=true, to_apply=%region_5.0 | all-reduce | flops 8 | bytes 64 | tf_op jit(solution)/shard_map/psum | solution.py:31
  71.1 5.7 %fusion.18 = f32[4,168,32]{1,2,0:T(8,128)S(1)} fusion(f32[4,168,32]{1,2,0:T(8,128)S(1)} %copy-done.6, f32[4,168,2048]{2,1,0:T(8,128)} %param.10, s32[2048]{0:T(1024)S(1)} %copy-done.7), kind=kOutput, calls=%fused_computation.36 | convolution fusion | flops 528569344 | bytes 5685248 | tf_op jit(solution)/shard_map/stg,gz->stz/dot_general | solution.py:71
  76.8 3.0 multiply_add_fusion.2
  79.8 2.4 copy-done.1
  82.2 22.3 %all-reduce.5.cloned.1.call-done = f32[24,2048]{1,0:T(8,128)} async-done(((f32[24,2048]{1,0:T(8,128)}), f32[24,2048]{1,0:T(8,128)}) %all-reduce.5.cloned.1.call-update) | async-done | bytes 196624 | tf_op jit(solution)/shard_map/psum | solution.py:32
  104.5 1.6 broadcast_divide_fusion.1
  106.1 90.5 %all-reduce.7.cloned.1.call-done = f32[8,24,2048]{2,0,1:T(8,128)} async-done(((f32[8,24,2048]{2,0,1:T(8,128)}), f32[8,24,2048]{2,0,1:T(8,128)}) %all-reduce.7.cloned.1.call-update) | async-done | bytes 1572880 | tf_op jit(solution)/shard_map/psum | solution.py:31
  196.5 2.5 fusion.16
  199.0 0.5 copy.14
  199.6 0.1 broadcast_in_dim.9
  199.7 2.9 fusion.12
  202.5 0.8 slice-done.4
  203.3 0.7 slice-done.1
  204.0 4.0 fusion.2
  208.0 3.0 convolution_subtract_fusion.1
  211.0 3.0 multiply_add_fusion.1
  214.1 0.4 slice.63
  214.5 0.5 fusion.11
  215.1 1.2 slice-done.2
  216.2 0.5 slice-done.3
  216.7 2.9 fusion.5
  219.6 3.0 convolution_subtract_fusion
  222.6 3.0 multiply_add_fusion
  225.6 0.5 fusion.10
  226.2 0.3 slice.66
  226.4 2.6 fusion.8
  229.1 2.4 copy-done.4
  231.5 0.1 fusion.61
  231.6 1.9 fusion.21
  233.5 0.7 copy.32
  234.3 3.3 fusion.19
  238.3 32.6 %psum.61 = f32[1]{0:T(128)} all-reduce(f32[1]{0:T(128)} %bitcast.10), channel_id=1, replica_groups=mesh['groups'=2,'branch'=2,'sub'=8] {'branch','sub'}, use_global_device_ids=true, to_apply=%region_9.10 | all-reduce | flops 1 | bytes 8 | tf_op jit(solution)/shard_map/psum | solution.py:62
  271.5 52.0 %all-reduce.9.cloned.1.call-done = f32[24,2048]{1,0:T(8,128)} async-done(((f32[24,2048]{1,0:T(8,128)}), f32[24,2048]{1,0:T(8,128)}) %all-reduce.9.cloned.1.call-update) | async-done | bytes 196624 | tf_op jit(solution)/shard_map/psum | solution.py:32
  323.6 1.6 broadcast_divide_fusion
  325.1 90.3 %all-reduce.11.cloned.1.call-done = f32[8,24,2048]{2,0,1:T(8,128)} async-done(((f32[8,24,2048]{2,0,1:T(8,128)}), f32[8,24,2048]{2,0,1:T(8,128)}) %all-reduce.11.cloned.1.call-update) | async-done | bytes 1572880 | tf_op jit(solution)/shard_map/psum | solution.py:31
  415.4 2.4 fusion.14
  417.8 0.2 broadcast_in_dim.10
  418.0 0.7 pad_maximum_fusion.1
  418.7 2.1 copy.15
  (39 shorter events, 0.3 us)
Async XLA Ops:
  7.2 9.6 %copy-start.11 = (s32[4]{0:T(128)S(1)}, s32[4]{0:T(128)}, u32[]{:S(2)}) copy-start(s32[4]{0:T(128)} %param.13) | copy-start | bytes 52
  7.2 10.2 %copy-start.12 = (s32[4]{0:T(128)S(1)}, s32[4]{0:T(128)}, u32[]{:S(2)}) copy-start(s32[4]{0:T(128)} %param.12) | copy-start | bytes 52
  7.2 63.9 %copy-start.7 = (s32[2048]{0:T(1024)S(1)}, s32[2048]{0:T(1024)}, u32[]{:S(2)}) copy-start(s32[2048]{0:T(1024)} %param.15) | copy-start | bytes 24580
  7.2 63.8 %copy-start.6 = (f32[4,168,32]{1,2,0:T(8,128)S(1)}, f32[4,168,32]{1,2,0:T(8,128)}, u32[]{:S(2)}) copy-start(f32[4,168,32]{1,2,0:T(8,128)} %param.19) | copy-start | bytes 258052
  7.2 97.3 %all-reduce.5.cloned.1.call-start = ((), (), s32[]{:S(2)}) async-start(), calls=%async_computation | async-start | bytes 393216 | tf_op jit(solution)/shard_map/psum | solution.py:32
  8.8 68.0 %copy-start.9 = (f32[2048]{0:T(1024)S(1)}, f32[2048]{0:T(1024)}, u32[]{:S(2)}) copy-start(f32[2048]{0:T(1024)} %param.18) | copy-start | bytes 24580
  8.8 68.0 %copy-start.10 = (f32[2048]{0:T(1024)S(1)}, f32[2048]{0:T(1024)}, u32[]{:S(2)}) copy-start(f32[2048]{0:T(1024)} %param.17) | copy-start | bytes 24580
  12.0 184.5 %all-reduce.7.cloned.1.call-start = ((), (), s32[]{:S(2)}) async-start(), calls=%async_computation.1 | async-start | bytes 3145728 | tf_op jit(solution)/shard_map/psum | solution.py:31
  16.7 306.8 %all-reduce.9.cloned.1.call-start = ((), (), s32[]{:S(2)}) async-start(), calls=%async_computation.2 | async-start | bytes 393216 | tf_op jit(solution)/shard_map/psum | solution.py:32
  71.0 5.7 %copy-start = (f32[4,168,2048]{2,1,0:T(8,128)S(1)}, f32[4,168,2048]{2,1,0:T(8,128)}, u32[]{:S(2)}) copy-start(f32[4,168,2048]{2,1,0:T(8,128)} %param.10) | copy-start | bytes 16515076
  79.8 2.4 copy-start.1
  82.2 117.4 %copy-start.5 = (f32[4,48,2048]{2,1,0:T(8,128)S(1)}, f32[4,48,2048]{2,1,0:T(8,128)}, u32[]{:S(2)}) copy-start(f32[4,48,2048]{2,1,0:T(8,128)} %param.11) | copy-start | bytes 4718596
  196.5 3.1 copy-start.2
  199.5 3.0 slice-start
  199.5 3.8 slice-start.4
  199.5 3.8 copy-start.8
  199.6 4.4 %slice-start.1 = ((s8[5505024]{0:T(1024)(128)(4,1)}), s8[1310720]{0:T(1024)(128)(4,1)S(1)}, s32[]{:S(2)}) async-start(s8[5505024]{0:T(1024)(128)(4,1)} %bitcast.41), calls=%async_computation.5 | async-start | bytes 2621440
  202.5 23.1 %copy-start.3 = (f32[4,48,2048]{2,1,0:T(8,128)}, f32[4,48,2048]{2,1,0:T(8,128)S(1)}, u32[]{:S(2)}) copy-start(f32[4,48,2048]{2,1,0:T(8,128)S(1)} %get-tuple-element.9) | copy-start | bytes 4718596
  214.0 2.2 slice-start.2
  214.5 2.2 slice-start.3
  229.1 2.4 copy-start.4
  234.3 181.1 %all-reduce.11.cloned.1.call-start = ((), (), s32[]{:S(2)}) async-start(), calls=%async_computation.3 | async-start | bytes 3145728 | tf_op jit(solution)/shard_map/psum | solution.py:31
Sparse Core Ops, SparseCore 0:
  12.1 92.3 all-reduce.4
  108.6 87.8 all-reduce.6
  234.4 89.0 all-reduce.8
  327.5 87.8 all-reduce.10
where the time goes:
time: 429 us; the launch traced here: 428 us
  waiting for transfers between devices  255 us (59%)
  blocking collectives  86.1 us (20%)
  matrix products  37.2 us (9%)
  other arithmetic  18.6 us (4%)
  between operations  16.5 us (4%)
  local copies, waits for them, and re-layouts  14.7 us (3%)
    psum x2, waiting for transfers between devices, average(): day_two, node_weight = lax.psum((day_two, node_weight), 'sub')  181 us
    psum x2, waiting for transfers between devices, average(): lax.psum((day_one, weight_sum, riding), ('branch', 'sub'))  74.3 us
    psum x1, blocking collectives, average(): lax.psum((day_one, weight_sum, riding), ('branch', 'sub'))  35.9 us
    psum x1, blocking collectives, shards(): dev_total = lax.psum(local_spread, ('branch', 'sub'))  32.6 us
    psum x1, blocking collectives, average(): day_two, node_weight = lax.psum((day_two, node_weight), 'sub')  17.6 us
    dot_general x3, matrix products, shards(): jnp.einsum('stg,gz->stz', current, zone_table, precision=lax.Precision.HI...  11.6 us
    min x3, other arithmetic, shards(): current = jnp.clip(current - step_size * gradient, 0.0, ceiling)  9.51 us
    unnamed x35, local copies, waits for them, and re-layouts  9.42 us
  transfers between devices with their start and end apart: 4, of which 4 were waited for; matrix products, arithmetic and copies ran while one was open for 5% of the time, Pallas kernels for 0%

commit v1 on v0

v1 whole, which is shorter than its diff:
```python
import functools

import jax
import jax.numpy as jnp
from jax import lax
from jax.experimental import pallas as pl
from jax.experimental.pallas import tpu as pltpu
from jax.sharding import PartitionSpec as P

DAY = 24
NODES_BR = 8
STEPS = 3
LANES = 128
EXTRA = 8

rho_value = 1.0
step_size = 0.3

MESH = pl.DeviceIdType.MESH


def kernel(
    n,
    zones_count,
    d_hbm,
    m_hbm,
    com_hbm,
    dem_ref,
    zone_ref,
    cap_ref,
    lin_ref,
    quad_ref,
    node_s,
    prob_s,
    out_d,
    out_m,
    out_a,
    out_dev,
    d_v,
    com_v,
    m_v,
    tab,
    tab_t,
    wt_all,
    recv2,
    back2,
    avg2,
    part1,
    pair1,
    recv1,
    back1,
    avg1,
    load_sem,
    store_sem,
    own_sem,
    wt_send,
    wt_recv,
    pair_send,
    pair_recv,
    send_sem,
    recv_sem,
):
    scen, hours, gens = d_v.shape
    section = m_v.shape[1]
    width = gens // n
    zones = zones_count
    balance = zones_count / gens
    me = lax.axis_index("sub")
    br = lax.axis_index("branch")
    day2 = pl.ds(DAY, DAY)

    def cols(i):
        return pl.ds(pl.multiple_of(i * width, LANES), width)

    loads = [
        pltpu.make_async_copy(d_hbm.at[:, pl.ds(0, section)], d_v.at[:, pl.ds(0, section)], load_sem.at[0]),
        pltpu.make_async_copy(
            d_hbm.at[:, pl.ds(section, hours - section)],
            d_v.at[:, pl.ds(section, hours - section)],
            load_sem.at[1],
        ),
        pltpu.make_async_copy(com_hbm, com_v, load_sem.at[2]),
        pltpu.make_async_copy(m_hbm, m_v, load_sem.at[3]),
    ]
    for load in loads:
        load.start()

    for j in range(scen):
        wt_all[me, j : j + 1, :] = jnp.full((1, LANES), prob_s[j].astype(jnp.float32), jnp.float32)
        wt_all[me, scen + j : scen + j + 1, :] = jnp.full(
            (1, LANES), node_s[j].astype(jnp.float32), jnp.float32
        )

    barrier = pltpu.get_barrier_semaphore()
    peers = [lax.rem(me + k, n) for k in range(1, n)]
    for peer in peers:
        pl.semaphore_signal(barrier, inc=1, device_id={"sub": peer}, device_id_type=MESH)
    pl.semaphore_signal(barrier, inc=1, device_id={"branch": 1 - br}, device_id_type=MESH)
    pl.semaphore_wait(barrier, n)

    def exchange(kind, src_of, dst):
        own = pltpu.make_async_copy(src_of(me), dst, own_sem.at[kind])
        own.start()
        copies = []
        for k, peer in enumerate(peers):
            copy = pltpu.make_async_remote_copy(
                src_ref=src_of(peer),
                dst_ref=dst,
                send_sem=send_sem.at[kind, k],
                recv_sem=recv_sem.at[kind, k],
                device_id={"sub": peer},
                device_id_type=MESH,
            )
            copy.start()
            copies.append(copy)
        return own, copies

    def arrive(flight):
        own, copies = flight
        own.wait()
        for copy in copies:
            copy.wait_recv()

    def left(flight):
        for copy in flight[1]:
            copy.wait_send()

    wt_copies = []
    for k, peer in enumerate(peers):
        copy = pltpu.make_async_remote_copy(
            src_ref=wt_all.at[me],
            dst_ref=wt_all.at[me],
            send_sem=wt_send.at[k],
            recv_sem=wt_recv.at[k],
            device_id={"sub": peer},
            device_id_type=MESH,
        )
        copy.start()
        wt_copies.append(copy)

    weights = [prob_s[j].astype(jnp.float32) for j in range(scen)]

    def pair(r):
        copy = pltpu.make_async_remote_copy(
            src_ref=part1.at[r],
            dst_ref=pair1.at[r],
            send_sem=pair_send.at[r],
            recv_sem=pair_recv.at[r],
            device_id={"branch": 1 - br},
            device_id_type=MESH,
        )
        copy.start()
        return copy

    def scatter2(r, src):
        return exchange(4 * r, lambda i: src.at[:, day2, cols(i)], recv2.at[r, me])

    def scatter1(r):
        return exchange(4 * r + 1, lambda i: pair1.at[r, :, cols(i)], recv1.at[r, me])

    def gather2(r):
        return exchange(4 * r + 2, lambda i: back2.at[r, i], avg2.at[r, :, :, cols(me)])

    def gather1(r):
        return exchange(4 * r + 3, lambda i: back1.at[r], avg1.at[r, :, cols(me)])

    def sum_day1(r):
        total = weights[0] * d_v[0, 0:DAY]
        for j in range(1, scen):
            total = total + weights[j] * d_v[j, 0:DAY]
        part1[r, 0:DAY] = total

    def mean1(r):
        total = recv1[r, 0]
        for q in range(1, n):
            total = total + recv1[r, q]
        if r == 0:
            weight = total[DAY : DAY + 1]
        else:
            weight = avg1[0, DAY : DAY + 1, 0:width]
        back1[r, 0:DAY] = total[0:DAY] / weight
        back1[r, DAY : DAY + EXTRA] = total[DAY : DAY + EXTRA]

    def mean2(r):
        for h in range(width // LANES):
            lane = slice(h * LANES, (h + 1) * LANES)

            def gather_sum(q, carry):
                sums, heft = list(carry[0]), list(carry[1])
                tile = wt_all[q]
                for j in range(scen):
                    x = recv2[r, q, j, :, lane]
                    w, node = tile[j : j + 1], tile[scen + j : scen + j + 1]
                    for key in range(NODES_BR):
                        part = jnp.where(node == float(key), w, 0.0)
                        sums[key] = sums[key] + part * x
                        heft[key] = heft[key] + part
                return tuple(sums), tuple(heft)

            zero = jnp.zeros((DAY, LANES), jnp.float32)
            row = jnp.zeros((1, LANES), jnp.float32)
            sums, heft = lax.fori_loop(
                0, n, gather_sum, ((zero,) * NODES_BR, (row,) * NODES_BR)
            )
            means = [sums[key] / heft[key] for key in range(NODES_BR)]

            def spread(q, carry):
                tile = wt_all[q]
                for j in range(scen):
                    node = tile[scen + j : scen + j + 1]
                    found = jnp.where(node == 0.0, 1.0, 0.0) * means[0]
                    for key in range(1, NODES_BR):
                        found = found + jnp.where(node == float(key), 1.0, 0.0) * means[key]
                    back2[r, q, j, :, lane] = found
                return carry

            lax.fori_loop(0, n, spread, 0)

    lane_id = lax.broadcasted_iota(jnp.int32, (1, LANES), 1)

    def sweeps(block, first, rows, base, slope):
        js, jn = block
        size = jn * rows
        view = (slice(js, js + jn), slice(first, first + rows))
        current = d_v[view].reshape(size, gens)
        demand = dem_ref[view].reshape(size, LANES)
        top = jnp.where(com_v[view].reshape(size, gens) > 0, cap_ref[...], 0.0)
        for sweep in range(STEPS):
            high = current.astype(jnp.bfloat16)
            low = (current - high.astype(jnp.float32)).astype(jnp.bfloat16)
            zone_sum = jnp.dot(high, tab[...], preferred_element_type=jnp.float32)
            zone_sum = zone_sum + jnp.dot(low, tab[...], preferred_element_type=jnp.float32)
            mismatch = (step_size * balance) * (zone_sum - demand)
            m_high = mismatch.astype(jnp.bfloat16).astype(jnp.float32)
            m_low = mismatch - m_high
            m_both = jnp.where(lane_id < zones, m_high, jnp.where(lane_id < 2 * zones, m_low, 0.0))
            feedback = jnp.dot(
                m_both.astype(jnp.bfloat16), tab_t[...], preferred_element_type=jnp.float32
            )
            current = jnp.minimum(jnp.maximum(slope * current - base - feedback, 0.0), top)
        d_v[view] = current.reshape(jn, rows, gens)

    lin = step_size * lin_ref[...]
    late_slope = 1.0 - step_size * quad_ref[...]
    early_slope = late_slope - step_size * rho_value

    def late(j):
        sweeps((j, 1), section, hours - section, lin, late_slope)
        copy = pltpu.make_async_copy(
            d_v.at[j, pl.ds(section, hours - section)],
            out_d.at[j, pl.ds(section, hours - section)],
            store_sem.at[j],
        )
        copy.start()
        return copy

    def early(first):
        pieces = []
        spread_sum = jnp.zeros((EXTRA, gens), jnp.float32)
        for j in range(scen):
            mean = avg1[0, 0:DAY] if first == 0 else avg2[0, j]
            gap = d_v[j, first : first + DAY] - mean
            changed = m_v[j, first : first + DAY] + rho_value * gap
            m_v[j, first : first + DAY] = changed
            square = (weights[j] * gap * gap).reshape(DAY // EXTRA, EXTRA, gens)
            spread_sum = spread_sum + jnp.sum(square, axis=0)
            pieces.append(lin + step_size * (changed - rho_value * mean))
        sweeps((0, scen), first, DAY, jnp.concatenate(pieces, axis=0), early_slope)
        return spread_sum

    flight2 = scatter2(0, d_hbm)
    loads[0].wait()
    sum_day1(0)
    part1[0, DAY : DAY + EXTRA] = jnp.full((EXTRA, gens), sum(weights), jnp.float32)
    copy = pair(0)
    ids = lax.broadcasted_iota(jnp.int32, (LANES, gens), 0) % zones
    one_hot = jnp.where(ids == zone_ref[...], 1.0, 0.0)
    tab_t[...] = one_hot.astype(jnp.bfloat16)
    tab[...] = one_hot.T.astype(jnp.bfloat16)
    copy.wait()
    pair1[0] = pair1[0] + part1[0]
    flight1 = scatter1(0)
    loads[1].wait()
    loads[2].wait()
    stores = [late(0)]
    arrive(flight1)
    mean1(0)
    back_flight1 = gather1(0)
    for copy in wt_copies:
        copy.wait()
    arrive(flight2)
    mean2(0)
    back_flight2 = gather2(0)
    loads[3].wait()
    stores.append(late(1))
    arrive(back_flight1)
    arrive(back_flight2)

    spread_two = early(DAY)
    second2 = scatter2(1, d_v)
    spread_one = early(0)
    sum_day1(1)
    part1[1, DAY : DAY + EXTRA] = spread_one + spread_two
    copy = pair(1)
    late_stores = [
        pltpu.make_async_copy(m_v, out_m, store_sem.at[scen]),
        pltpu.make_async_copy(
            d_v.at[:, pl.ds(0, section)], out_d.at[:, pl.ds(0, section)], store_sem.at[scen + 1]
        ),
    ]
    for store in late_stores:
        store.start()
    copy.wait()
    pair1[1] = pair1[1] + part1[1]
    second1 = scatter1(1)
    for j in range(2, scen - 1):
        stores.append(late(j))
    arrive(second1)
    mean1(1)
    back_second1 = gather1(1)
    arrive(second2)
    mean2(1)
    back_second2 = gather2(1)
    for j in range(scen - 1, scen):
        stores.append(late(j))
    arrive(back_second1)
    for j in range(scen):
        store = pltpu.make_async_copy(
            avg1.at[1, pl.ds(0, DAY)], out_a.at[j, pl.ds(0, DAY)], store_sem.at[scen + 2 + j]
        )
        store.start()
        stores.append(store)
    total = jnp.sum(avg1[1, DAY : DAY + EXTRA], keepdims=True)
    weight = avg1[0, DAY : DAY + 1, 0:1]
    out_dev[...] = jnp.broadcast_to(total / (weight * (section * gens)), out_dev.shape)
    arrive(back_second2)
    store = pltpu.make_async_copy(avg2.at[1], out_a.at[:, day2], store_sem.at[2 * scen + 2])
    store.start()
    stores.append(store)
    for flight in (
        flight1, flight2, back_flight1, back_flight2, second1, second2, back_second1, back_second2
    ):
        left(flight)
    for store in stores + late_stores:
        store.wait()


def shards(
    n,
    dispatch,
    multiplier,
    node_of,
    prob_weight,
    commitment,
    zone_of,
    capacity,
    linear_cost,
    quad_cost,
    demand,
):
    scen, hours, gens = dispatch.shape
    section = multiplier.shape[1]
    width = gens // n
    copies = LANES // demand.shape[2]
    wide = jnp.tile(demand, (1, 1, copies))
    any_spec = pl.BlockSpec(memory_space=pl.ANY)
    vmem = pl.BlockSpec(memory_space=pltpu.VMEM)
    smem = pl.BlockSpec(memory_space=pltpu.SMEM)
    f32 = jnp.float32
    dma = pltpu.SemaphoreType.DMA
    new_dispatch, new_multiplier, next_average, deviation = pl.pallas_call(
        functools.partial(kernel, n, demand.shape[2]),
        out_shape=(
            jax.ShapeDtypeStruct(dispatch.shape, f32),
            jax.ShapeDtypeStruct(multiplier.shape, f32),
            jax.ShapeDtypeStruct(multiplier.shape, f32),
            jax.ShapeDtypeStruct((8, LANES), f32),
        ),
        in_specs=[any_spec] * 3 + [vmem] * 5 + [smem] * 2,
        out_specs=(any_spec, any_spec, any_spec, vmem),
        scratch_shapes=[
            pltpu.VMEM((scen, hours, gens), f32),
            pltpu.VMEM((scen, hours, gens), jnp.int32),
            pltpu.VMEM((scen, section, gens), f32),
            pltpu.VMEM((gens, LANES), jnp.bfloat16),
            pltpu.VMEM((LANES, gens), jnp.bfloat16),
            pltpu.VMEM((n, 8, LANES), f32),
            pltpu.VMEM((2, n, scen, DAY, width), f32),
            pltpu.VMEM((2, n, scen, DAY, width), f32),
            pltpu.VMEM((2, scen, DAY, gens), f32),
            pltpu.VMEM((2, DAY + EXTRA, gens), f32),
            pltpu.VMEM((2, DAY + EXTRA, gens), f32),
            pltpu.VMEM((2, n, DAY + EXTRA, width), f32),
            pltpu.VMEM((2, DAY + EXTRA, width), f32),
            pltpu.VMEM((2, DAY + EXTRA, gens), f32),
            dma((4,)),
            dma((2 * scen + 3,)),
            dma((8,)),
            dma((n - 1,)),
            dma((n - 1,)),
            dma((2,)),
            dma((2,)),
            dma((8, n - 1)),
            dma((8, n - 1)),
        ],
        compiler_params=pltpu.CompilerParams(
            collective_id=0, has_side_effects=True, vmem_limit_bytes=56 * 1024 * 1024
        ),
    )(
        dispatch,
        multiplier,
        commitment,
        wide,
        zone_of[None],
        capacity[None],
        linear_cost[None],
        quad_cost[None],
        node_of,
        prob_weight,
    )
    return new_dispatch, new_multiplier, next_average, deviation[0, :1]


def solution(mesh):
    spread = ("groups", "branch", "sub")
    in_specs = (
        P(spread, None, None),
        P(spread, None, None),
        P(spread),
        P(spread),
        P(spread, None, None),
        P(),
        P(),
        P(),
        P(),
        P(spread, None, None),
    )
    out_specs = (P(spread, None, None), P(spread, None, None), P(spread, None, None), P("groups"))
    return jax.shard_map(
        functools.partial(shards, mesh.shape["sub"]),
        mesh=mesh,
        in_specs=in_specs,
        out_specs=out_specs,
        check_vma=False,
    )
```

time: 429 us -> 121 us (0.28)
  waiting for transfers between devices: 255 us -> 0 us
  Pallas kernels: 0 us -> 107 us
  blocking collectives: 86.1 us -> 0 us
  matrix products: 37.2 us -> 0 us
  other arithmetic: 18.6 us -> 0 us
  between operations: 16.5 us -> 0.65 us
    psum x4 -> x0, waiting for transfers between devices: 255 us -> none  [the longest x2 181 us: average(): day_two, node_weight = lax.psum((day_two, node_weight), 'sub')]
    pallas_call x0 -> x1, Pallas kernels: none -> 107 us  [shards(): pl.pallas_call(functools.partial(kernel, n, demand.shape[2]), out_shape=(...]
    psum x3 -> x0, blocking collectives: 86.1 us -> none  [the longest x1 35.9 us: average(): lax.psum((day_one, weight_sum, riding), ('branch', 'sub'))]
    dot_general x12 -> x0, matrix products: 37.2 us -> none  [the longest x3 11.6 us: shards(): jnp.einsum('stg,gz->stz', current, zone_table, precision=lax.Precision.HI...]
    min x3 -> x0, other arithmetic: 9.51 us -> none  [shards(): current = jnp.clip(current - step_size * gradient, 0.0, ceiling)]
    unnamed x35 -> x7, local copies, waits for them, and re-layouts: 9.42 us -> 8.93 us
  transfers between devices with their start and end apart: 4 -> 0, of which waited for: 4 -> 0; matrix products, arithmetic and copies ran while one was open for 5% -> 0% of each run, Pallas kernels for 0% -> 0%
where the time goes in v1:
time: 121 us; the launch traced here: 120 us
  Pallas kernels  107 us (88%)
  local copies, waits for them, and re-layouts  12 us (10%)
    pallas_call x1, Pallas kernels, shards(): pl.pallas_call(functools.partial(kernel, n, demand.shape[2]), out_shape=(...  107 us
    unnamed x7, local copies, waits for them, and re-layouts  8.93 us

profile of v1, /device:TPU:0, one launch (start us, length us, event | category | flops | bytes accessed | tf_op | source)
XLA Modules:
  0.0 119.7 jit_solution(14286353422905219608)
XLA Ops:
  0.6 0.9 tile.4
  1.6 0.9 copy.15.dem_ref
  2.5 107.0 %shard_map.129 = (f32[4,168,2048]{2,1,0:T(8,128)}, f32[4,48,2048]{2,1,0:T(8,128)}, f32[4,48,2048]{2,1,0:T(8,128)}, f32[8,128]{1,0:T(8,128)}) custom-call(f32[4,168,2048]{2,1,0:T(8,128)} %d_hbm.1, f32[4,48,2048]{2,1,0:T(8,128)} %m_hbm.1, s32[4,168,2048]{2,1,0:T(8,128)} %com_hbm.1, f32[4,168,128]{2,1,0:T(8,128)} %copy.15.dem_ref, s32[1,2048]{1,0:T(1,128)} %bitcast.7, ...), custom_call_target="tpu_custom_call" | custom-call | tf_op jit(solution)/shard_map/pallas_call | solution.py:371
  109.6 1.2 slice.3
  110.8 0.0 copy-start.1
  110.8 5.8 %copy.19 = f32[4,168,2048]{2,1,0:T(8,128)} copy(f32[4,168,2048]{2,1,0:T(8,128)} %get-tuple-element.16) | data formatting | bytes 11010048
  116.6 0.0 copy-done.1
  116.6 0.0 copy-start
  116.6 1.1 copy.20
  117.7 0.8 copy-done
  118.5 1.1 copy.21
Async XLA Ops:
  110.8 5.8 %copy-start.1 = (f32[4,48,2048]{2,1,0:T(8,128)S(1)}, f32[4,48,2048]{2,1,0:T(8,128)}, u32[]{:S(2)}) copy-start(f32[4,48,2048]{2,1,0:T(8,128)} %get-tuple-element.17) | copy-start | bytes 4718596
  116.6 2.0 %copy-start = (f32[4,48,2048]{2,1,0:T(8,128)S(1)}, f32[4,48,2048]{2,1,0:T(8,128)}, u32[]{:S(2)}) copy-start(f32[4,48,2048]{2,1,0:T(8,128)} %get-tuple-element.18) | copy-start | bytes 4718596

commit v2 on v1

v2 whole, which is shorter than its diff:
```python
import functools

import jax
import jax.numpy as jnp
from jax import lax
from jax.experimental import pallas as pl
from jax.experimental.pallas import tpu as pltpu
from jax.sharding import PartitionSpec as P

DAY = 24
NODES_BR = 8
STEPS = 3
LANES = 128
EXTRA = 8

rho_value = 1.0
step_size = 0.3

MESH = pl.DeviceIdType.MESH


def kernel(
    n,
    zones,
    d_hbm,
    m_hbm,
    com_hbm,
    dem_ref,
    zone_ref,
    cap_ref,
    lin_ref,
    quad_ref,
    node_s,
    prob_s,
    out_d,
    out_m,
    out_a,
    out_dev,
    d_v,
    com_v,
    m_v,
    tab,
    tab_t,
    wt_all,
    dev_all,
    inv_node,
    swap2,
    own2,
    low2,
    high2,
    back2,
    avg2,
    swap1,
    own1,
    low1,
    high1,
    part1,
    pair1,
    avg1,
    load_sem,
    store_sem,
    tile_send,
    tile_recv,
    pair_send,
    pair_recv,
    swap_send,
    swap_recv,
    low_send,
    low_recv,
    high_send,
    high_recv,
    back_send,
    back_recv,
):
    scen, hours, gens = d_v.shape
    section = m_v.shape[1]
    chunks = gens // (2 * LANES)
    half = gens // 2
    balance = zones / gens
    me = lax.axis_index("sub")
    br = lax.axis_index("branch")
    side = lax.rem(me, 2)
    partner = me + 1 - 2 * side
    line = me // 2
    length = n // 2
    first_end, last_end = line == 0, line == length - 1
    middle = jnp.logical_and(line > 0, line < length - 1)
    place = br * n + me
    day2 = pl.ds(DAY, DAY)

    def lanes(owner, c):
        return pl.ds(pl.multiple_of(owner * half + c * LANES, LANES), LANES)

    def half_of(owner):
        return pl.ds(pl.multiple_of(owner * half, LANES), half)

    loads = [
        pltpu.make_async_copy(d_hbm.at[:, pl.ds(0, section)], d_v.at[:, pl.ds(0, section)], load_sem.at[0]),
        pltpu.make_async_copy(
            d_hbm.at[:, pl.ds(section, hours - section)],
            d_v.at[:, pl.ds(section, hours - section)],
            load_sem.at[1],
        ),
        pltpu.make_async_copy(com_hbm, com_v, load_sem.at[2]),
        pltpu.make_async_copy(m_hbm, m_v, load_sem.at[3]),
    ]
    for load in loads:
        load.start()

    for j in range(scen):
        wt_all[place, j : j + 1, :] = jnp.full((1, LANES), prob_s[j].astype(jnp.float32), jnp.float32)
        wt_all[place, scen + j : scen + j + 1, :] = jnp.full(
            (1, LANES), node_s[j].astype(jnp.float32), jnp.float32
        )

    others = [
        (lax.rem(br + flip, 2), lax.rem(me + k, n))
        for flip in range(2)
        for k in range(n)
        if flip or k
    ]
    barrier = pltpu.get_barrier_semaphore()
    for to_br, to_sub in others:
        pl.semaphore_signal(
            barrier, inc=1, device_id={"branch": to_br, "sub": to_sub}, device_id_type=MESH
        )
    pl.semaphore_wait(barrier, len(others))

    def remote(src, dst, send, recv, target):
        return pltpu.make_async_remote_copy(
            src_ref=src,
            dst_ref=dst,
            send_sem=send,
            recv_sem=recv,
            device_id=target,
            device_id_type=MESH,
        )

    def tiles(r, table):
        copies = []
        for k, (to_br, to_sub) in enumerate(others):
            copy = remote(
                table.at[place],
                table.at[place],
                tile_send.at[r, k],
                tile_recv.at[r, k],
                {"branch": to_br, "sub": to_sub},
            )
            copy.start()
            copies.append(copy)
        return copies

    weights = [prob_s[j].astype(jnp.float32) for j in range(scen)]

    def pair(r):
        copy = remote(
            part1.at[r], pair1.at[r], pair_send.at[r], pair_recv.at[r], {"branch": 1 - br}
        )
        copy.start()
        return copy

    def swap(r, c, src):
        if c < chunks:
            source, target = src.at[:, day2, lanes(1 - side, c)], swap2.at[r, c]
        else:
            source, target = pair1.at[r, :, half_of(1 - side)], swap1.at[r]
        return remote(source, target, swap_send.at[r, c], swap_recv.at[r, c], {"sub": partner})

    def buffers(r, c):
        if c < chunks:
            return own2.at[r, c], low2.at[r, c], high2.at[r, c]
        return own1.at[r], low1.at[r], high1.at[r]

    def upward(r, c):
        _, low, _ = buffers(r, c)
        return remote(low, low, low_send.at[r, c], low_recv.at[r, c], {"sub": lax.rem(me + 2, n)})

    def downward(r, c):
        own, _, high = buffers(r, c)
        return remote(
            own, high, high_send.at[r, c], high_recv.at[r, c], {"sub": lax.rem(me + n - 2, n)}
        )

    def back(r, c):
        if c < chunks:
            source, target = back2.at[r, c], avg2.at[r, :, :, lanes(side, c)]
        else:
            source = target = avg1.at[r, :, half_of(side)]
        return remote(source, target, back_send.at[r, c], back_recv.at[r, c], {"sub": partner})

    def masked(tile, j, key, value):
        return jnp.where(tile[scen + j : scen + j + 1] == float(key), value, 0.0)

    def begin(r, c, src):
        swap(r, c, src).wait_recv()
        own, low, high = buffers(r, c)
        if c < chunks:
            sums = [jnp.zeros((DAY, LANES), jnp.float32)] * NODES_BR
            for mine in (True, False):
                tile = wt_all[place if mine else br * n + partner]
                for j in range(scen):
                    own_x = d_v[j, DAY : 2 * DAY, lanes(side, c)] if mine else swap2[r, c, j]
                    for key in range(NODES_BR):
                        sums[key] = sums[key] + masked(tile, j, key, tile[j : j + 1]) * own_x
            for key in range(NODES_BR):
                own[key] = sums[key]
        else:
            own[...] = pair1[r, :, half_of(side)] + swap1[r]

        @pl.when(first_end)
        def _():
            low[...] = own[...]
            upward(r, c).start()

        @pl.when(last_end)
        def _():
            high[...] = jnp.zeros(high.shape, jnp.float32)
            downward(r, c).start()

    def finish(r, c):
        own, low, high = buffers(r, c)

        @pl.when(jnp.logical_not(first_end))
        def _():
            upward(r, c).wait_recv()
            low[...] = low[...] + own[...]

        @pl.when(middle)
        def _():
            upward(r, c).start()

        @pl.when(jnp.logical_not(last_end))
        def _():
            downward(r, c).wait_recv()

        @pl.when(middle)
        def _():
            own[...] = own[...] + high[...]
            downward(r, c).start()

        if c < chunks:
            means = [
                (low[key] + high[key]) * inv_node[key : key + 1] for key in range(NODES_BR)
            ]
            for which in range(2):
                tile = wt_all[place if which == 0 else br * n + partner]
                for j in range(scen):
                    found = masked(tile, j, 0, means[0])
                    for key in range(1, NODES_BR):
                        found = found + masked(tile, j, key, means[key])
                    if which == 0:
                        avg2[r, j, :, lanes(side, c)] = found
                    else:
                        back2[r, c, j] = found
        else:
            avg1[r, :, half_of(side)] = (low[...] + high[...]) * inv_node[NODES_BR, 0]
        back(r, c).start()

    def settle(r):
        for c in range(chunks + 1):
            swap(r, c, d_hbm if r == 0 else d_v).wait_send()
            back(r, c).wait_send()

            @pl.when(jnp.logical_not(last_end))
            def _():
                upward(r, c).wait_send()

            @pl.when(jnp.logical_not(first_end))
            def _():
                downward(r, c).wait_send()

    def chain(r, src):
        lag = 3
        for c in range(chunks + 1 + lag):
            if c < chunks + 1:
                begin(r, c, src)
            if c >= lag:
                finish(r, c - lag)

    def sum_day1(r):
        total = weights[0] * d_v[0, 0:DAY]
        for j in range(1, scen):
            total = total + weights[j] * d_v[j, 0:DAY]
        part1[r] = total

    lane_id = lax.broadcasted_iota(jnp.int32, (1, LANES), 1)

    def sweeps(block, first, rows, base, slope):
        js, jn = block
        size = jn * rows
        view = (slice(js, js + jn), slice(first, first + rows))
        current = d_v[view].reshape(size, gens)
        demand = dem_ref[view].reshape(size, LANES)
        top = jnp.where(com_v[view].reshape(size, gens) > 0, cap_ref[...], 0.0)
        for sweep in range(STEPS):
            high = current.astype(jnp.bfloat16)
            low = (current - high.astype(jnp.float32)).astype(jnp.bfloat16)
            zone_sum = jnp.dot(high, tab[...], preferred_element_type=jnp.float32)
            zone_sum = zone_sum + jnp.dot(low, tab[...], preferred_element_type=jnp.float32)
            mismatch = (step_size * balance) * (zone_sum - demand)
            m_high = mismatch.astype(jnp.bfloat16).astype(jnp.float32)
            m_low = mismatch - m_high
            m_both = jnp.where(lane_id < zones, m_high, jnp.where(lane_id < 2 * zones, m_low, 0.0))
            feedback = jnp.dot(
                m_both.astype(jnp.bfloat16), tab_t[...], preferred_element_type=jnp.float32
            )
            current = jnp.minimum(jnp.maximum(slope * current - base - feedback, 0.0), top)
        d_v[view] = current.reshape(jn, rows, gens)

    lin = step_size * lin_ref[...]
    late_slope = 1.0 - step_size * quad_ref[...]
    early_slope = late_slope - step_size * rho_value

    def late(j):
        sweeps((j, 1), section, hours - section, lin, late_slope)
        copy = pltpu.make_async_copy(
            d_v.at[j, pl.ds(section, hours - section)],
            out_d.at[j, pl.ds(section, hours - section)],
            store_sem.at[j],
        )
        copy.start()
        return copy

    def early(first):
        pieces = []
        spread_sum = jnp.zeros((EXTRA, gens), jnp.float32)
        for j in range(scen):
            mean = avg1[0] if first == 0 else avg2[0, j]
            gap = d_v[j, first : first + DAY] - mean
            changed = m_v[j, first : first + DAY] + rho_value * gap
            m_v[j, first : first + DAY] = changed
            square = (weights[j] * gap * gap).reshape(DAY // EXTRA, EXTRA, gens)
            spread_sum = spread_sum + jnp.sum(square, axis=0)
            pieces.append(lin + step_size * (changed - rho_value * mean))
        sweeps((0, scen), first, DAY, jnp.concatenate(pieces, axis=0), early_slope)
        return spread_sum

    for c in range(chunks):
        swap(0, c, d_hbm).start()
    wt_copies = tiles(0, wt_all)
    loads[0].wait()
    sum_day1(0)
    copy = pair(0)
    ids = lax.broadcasted_iota(jnp.int32, (LANES, gens), 0) % zones
    one_hot = jnp.where(ids == zone_ref[...], 1.0, 0.0)
    tab_t[...] = one_hot.astype(jnp.bfloat16)
    tab[...] = one_hot.T.astype(jnp.bfloat16)
    for tile_copy in wt_copies:
        tile_copy.wait()
    heft = [jnp.zeros((1, LANES), jnp.float32)] * NODES_BR
    for q in range(n):
        tile = wt_all[br * n + q]
        for j in range(scen):
            for key in range(NODES_BR):
                heft[key] = heft[key] + masked(tile, j, key, tile[j : j + 1])
    for key in range(NODES_BR):
        inv_node[key : key + 1] = 1.0 / heft[key]
    weight_sum = jnp.zeros((1, LANES), jnp.float32)
    for q in range(2 * n):
        for j in range(scen):
            weight_sum = weight_sum + wt_all[q, j : j + 1]
    inv_node[NODES_BR : NODES_BR + 1] = 1.0 / weight_sum
    copy.wait()
    pair1[0] = pair1[0] + part1[0]
    swap(0, chunks, d_hbm).start()
    chain(0, d_hbm)
    loads[1].wait()
    loads[2].wait()
    loads[3].wait()
    stores = [late(0)]
    for c in range(chunks + 1):
        back(0, c).wait_recv()

    spread_two = early(DAY)
    for c in range(chunks):
        swap(1, c, d_v).start()
    spread_one = early(0)
    sum_day1(1)
    copy = pair(1)
    spread_all = spread_one + spread_two
    spread_tile = spread_all[:, 0:LANES]
    for k in range(1, gens // LANES):
        spread_tile = spread_tile + spread_all[:, k * LANES : (k + 1) * LANES]
    dev_all[place] = spread_tile
    dev_copies = tiles(1, dev_all)
    late_stores = [
        pltpu.make_async_copy(m_v, out_m, store_sem.at[scen]),
        pltpu.make_async_copy(
            d_v.at[:, pl.ds(0, section)], out_d.at[:, pl.ds(0, section)], store_sem.at[scen + 1]
        ),
    ]
    for store in late_stores:
        store.start()
    copy.wait()
    pair1[1] = pair1[1] + part1[1]
    swap(1, chunks, d_v).start()
    chain(1, d_v)
    for j in range(1, scen):
        stores.append(late(j))
    for c in range(chunks + 1):
        back(1, c).wait_recv()
    for j in range(scen):
        store = pltpu.make_async_copy(
            avg1.at[1], out_a.at[j, pl.ds(0, DAY)], store_sem.at[scen + 2 + j]
        )
        store.start()
        stores.append(store)
    store = pltpu.make_async_copy(avg2.at[1], out_a.at[:, day2], store_sem.at[2 * scen + 2])
    store.start()
    stores.append(store)
    for copy in dev_copies:
        copy.wait()
    total = dev_all[0]
    for q in range(1, 2 * n):
        total = total + dev_all[q]
    total = jnp.sum(total, keepdims=True)
    out_dev[...] = jnp.broadcast_to(total / (weight_sum[:, 0:1] * (section * gens)), out_dev.shape)
    settle(0)
    settle(1)
    for store in stores + late_stores:
        store.wait()


def shards(
    n,
    dispatch,
    multiplier,
    node_of,
    prob_weight,
    commitment,
    zone_of,
    capacity,
    linear_cost,
    quad_cost,
    demand,
):
    scen, hours, gens = dispatch.shape
    section = multiplier.shape[1]
    chunks = gens // (2 * LANES)
    copies = LANES // demand.shape[2]
    wide = jnp.tile(demand, (1, 1, copies))
    any_spec = pl.BlockSpec(memory_space=pl.ANY)
    vmem = pl.BlockSpec(memory_space=pltpu.VMEM)
    smem = pl.BlockSpec(memory_space=pltpu.SMEM)
    f32 = jnp.float32
    dma = pltpu.SemaphoreType.DMA
    new_dispatch, new_multiplier, next_average, deviation = pl.pallas_call(
        functools.partial(kernel, n, demand.shape[2]),
        out_shape=(
            jax.ShapeDtypeStruct(dispatch.shape, f32),
            jax.ShapeDtypeStruct(multiplier.shape, f32),
            jax.ShapeDtypeStruct(multiplier.shape, f32),
            jax.ShapeDtypeStruct((8, LANES), f32),
        ),
        in_specs=[any_spec] * 3 + [vmem] * 5 + [smem] * 2,
        out_specs=(any_spec, any_spec, any_spec, vmem),
        scratch_shapes=[
            pltpu.VMEM((scen, hours, gens), f32),
            pltpu.VMEM((scen, hours, gens), jnp.int32),
            pltpu.VMEM((scen, section, gens), f32),
            pltpu.VMEM((gens, LANES), jnp.bfloat16),
            pltpu.VMEM((LANES, gens), jnp.bfloat16),
            pltpu.VMEM((2 * n, 8, LANES), f32),
            pltpu.VMEM((2 * n, 8, LANES), f32),
            pltpu.VMEM((2 * NODES_BR, LANES), f32),
            pltpu.VMEM((2, chunks, scen, DAY, LANES), f32),
            pltpu.VMEM((2, chunks, NODES_BR, DAY, LANES), f32),
            pltpu.VMEM((2, chunks, NODES_BR, DAY, LANES), f32),
            pltpu.VMEM((2, chunks, NODES_BR, DAY, LANES), f32),
            pltpu.VMEM((2, chunks, scen, DAY, LANES), f32),
            pltpu.VMEM((2, scen, DAY, gens), f32),
            pltpu.VMEM((2, DAY, gens // 2), f32),
            pltpu.VMEM((2, DAY, gens // 2), f32),
            pltpu.VMEM((2, DAY, gens // 2), f32),
            pltpu.VMEM((2, DAY, gens // 2), f32),
            pltpu.VMEM((2, DAY, gens), f32),
            pltpu.VMEM((2, DAY, gens), f32),
            pltpu.VMEM((2, DAY, gens), f32),
            dma((4,)),
            dma((2 * scen + 3,)),
            dma((2, 2 * n - 1)),
            dma((2, 2 * n - 1)),
            dma((2,)),
            dma((2,)),
        ]
        + [dma((2, chunks + 1))] * 8,
        compiler_params=pltpu.CompilerParams(
            collective_id=0, has_side_effects=True, vmem_limit_bytes=56 * 1024 * 1024
        ),
    )(
        dispatch,
        multiplier,
        commitment,
        wide,
        zone_of[None],
        capacity[None],
        linear_cost[None],
        quad_cost[None],
        node_of,
        prob_weight,
    )
    return new_dispatch, new_multiplier, next_average, deviation[0, :1]


def solution(mesh):
    spread = ("groups", "branch", "sub")
    in_specs = (
        P(spread, None, None),
        P(spread, None, None),
        P(spread),
        P(spread),
        P(spread, None, None),
        P(),
        P(),
        P(),
        P(),
        P(spread, None, None),
    )
    out_specs = (P(spread, None, None), P(spread, None, None), P(spread, None, None), P("groups"))
    return jax.shard_map(
        functools.partial(shards, mesh.shape["sub"]),
        mesh=mesh,
        in_specs=in_specs,
        out_specs=out_specs,
        check_vma=False,
    )
```

time: 121 us -> 205 us (1.69)
  Pallas kernels: 107 us -> 192 us
    pallas_call x1, Pallas kernels: 107 us -> 192 us  [shards(): pl.pallas_call(functools.partial(kernel, n, demand.shape[2]), out_shape=(...]
where the time goes in v2:
time: 205 us; the launch traced here: 204 us
  Pallas kernels  192 us (94%)
  local copies, waits for them, and re-layouts  12 us (6%)
    pallas_call x1, Pallas kernels, shards(): pl.pallas_call(functools.partial(kernel, n, demand.shape[2]), out_shape=(...  192 us
    unnamed x7, local copies, waits for them, and re-layouts  8.93 us

profile of v2, /device:TPU:0, one launch (start us, length us, event | category | flops | bytes accessed | tf_op | source)
XLA Modules:
  0.0 204.5 jit_solution(15766690979345298116)
XLA Ops:
  0.6 0.9 tile.4
  1.6 0.9 copy.15.dem_ref
  2.5 191.8 %shard_map.129 = (f32[4,168,2048]{2,1,0:T(8,128)}, f32[4,48,2048]{2,1,0:T(8,128)}, f32[4,48,2048]{2,1,0:T(8,128)}, f32[8,128]{1,0:T(8,128)}) custom-call(f32[4,168,2048]{2,1,0:T(8,128)} %d_hbm.1, f32[4,48,2048]{2,1,0:T(8,128)} %m_hbm.1, s32[4,168,2048]{2,1,0:T(8,128)} %com_hbm.1, f32[4,168,128]{2,1,0:T(8,128)} %copy.15.dem_ref, s32[1,2048]{1,0:T(1,128)} %bitcast.7, ...), custom_call_target="tpu_custom_call" | custom-call | tf_op jit(solution)/shard_map/pallas_call | solution.py:447
  194.3 1.2 slice.3
  195.5 0.0 copy-start.1
  195.5 5.8 %copy.19 = f32[4,168,2048]{2,1,0:T(8,128)} copy(f32[4,168,2048]{2,1,0:T(8,128)} %get-tuple-element.16) | data formatting | bytes 11010048
  201.3 0.0 copy-done.1
  201.3 0.0 copy-start
  201.3 1.1 copy.20
  202.5 0.8 copy-done
  203.3 1.1 copy.21
Async XLA Ops:
  195.5 5.8 %copy-start.1 = (f32[4,48,2048]{2,1,0:T(8,128)S(1)}, f32[4,48,2048]{2,1,0:T(8,128)}, u32[]{:S(2)}) copy-start(f32[4,48,2048]{2,1,0:T(8,128)} %get-tuple-element.17) | copy-start | bytes 4718596
  201.3 2.0 copy-start

commit v3 on v2

--- a/solution.py
+++ b/solution.py
@@ -48,12 +48,14 @@
     own2,
     low2,
     high2,
+    rest2,
     back2,
     avg2,
     swap1,
     own1,
     low1,
     high1,
+    rest1,
     part1,
     pair1,
     avg1,
@@ -168,17 +170,17 @@
 
     def buffers(r, c):
         if c < chunks:
-            return own2.at[r, c], low2.at[r, c], high2.at[r, c]
-        return own1.at[r], low1.at[r], high1.at[r]
+            return own2.at[r, c], low2.at[r, c], high2.at[r, c], rest2.at[r, c]
+        return own1.at[r], low1.at[r], high1.at[r], rest1.at[r]
 
     def upward(r, c):
-        _, low, _ = buffers(r, c)
+        _, low, _, _ = buffers(r, c)
         return remote(low, low, low_send.at[r, c], low_recv.at[r, c], {"sub": lax.rem(me + 2, n)})
 
     def downward(r, c):
-        own, _, high = buffers(r, c)
+        _, _, high, rest = buffers(r, c)
         return remote(
-            own, high, high_send.at[r, c], high_recv.at[r, c], {"sub": lax.rem(me + n - 2, n)}
+            rest, high, high_send.at[r, c], high_recv.at[r, c], {"sub": lax.rem(me + n - 2, n)}
         )
 
     def back(r, c):
@@ -193,7 +195,7 @@
 
     def begin(r, c, src):
         swap(r, c, src).wait_recv()
-        own, low, high = buffers(r, c)
+        own, low, high, rest = buffers(r, c)
         if c < chunks:
             sums = [jnp.zeros((DAY, LANES), jnp.float32)] * NODES_BR
             for mine in (True, False):
@@ -215,29 +217,38 @@
         @pl.when(last_end)
         def _():
             high[...] = jnp.zeros(high.shape, jnp.float32)
+            rest[...] = own[...]
             downward(r, c).start()
 
-    def finish(r, c):
-        own, low, high = buffers(r, c)
-
-        @pl.when(jnp.logical_not(first_end))
+    lower = line < length // 2
+    upper = jnp.logical_not(lower)
+
+    def go_up(r, c, when):
+        own, low, _, _ = buffers(r, c)
+
+        @pl.when(jnp.logical_and(when, jnp.logical_not(first_end)))
         def _():
             upward(r, c).wait_recv()
             low[...] = low[...] + own[...]
 
-        @pl.when(middle)
+        @pl.when(jnp.logical_and(when, middle))
         def _():
             upward(r, c).start()
 
-        @pl.when(jnp.logical_not(last_end))
+    def go_down(r, c, when):
+        own, _, high, rest = buffers(r, c)
+
+        @pl.when(jnp.logical_and(when, jnp.logical_not(last_end)))
         def _():
             downward(r, c).wait_recv()
 
-        @pl.when(middle)
+        @pl.when(jnp.logical_and(when, middle))
         def _():
-            own[...] = own[...] + high[...]
+            rest[...] = own[...] + high[...]
             downward(r, c).start()
 
+    def finish(r, c):
+        own, low, high, _ = buffers(r, c)
         if c < chunks:
             means = [
                 (low[key] + high[key]) * inv_node[key : key + 1] for key in range(NODES_BR)
@@ -269,13 +280,20 @@
             def _():
                 downward(r, c).wait_send()
 
-    def chain(r, src):
-        lag = 3
-        for c in range(chunks + 1 + lag):
-            if c < chunks + 1:
+    def chain(r, src, pieces):
+        near, far = 1, 5
+        for c in range(chunks + 1 + far):
+            if c <= chunks:
                 begin(r, c, src)
-            if c >= lag:
-                finish(r, c - lag)
+            if 0 <= c - near <= chunks:
+                go_up(r, c - near, lower)
+                go_down(r, c - near, upper)
+            if c >= far:
+                go_up(r, c - far, upper)
+                go_down(r, c - far, lower)
+                finish(r, c - far)
+            if c >= 3 and c - 3 < len(pieces):
+                pieces[c - 3]()
 
     def sum_day1(r):
         total = weights[0] * d_v[0, 0:DAY]
@@ -311,15 +329,20 @@
     late_slope = 1.0 - step_size * quad_ref[...]
     early_slope = late_slope - step_size * rho_value
 
-    def late(j):
-        sweeps((j, 1), section, hours - section, lin, late_slope)
-        copy = pltpu.make_async_copy(
-            d_v.at[j, pl.ds(section, hours - section)],
-            out_d.at[j, pl.ds(section, hours - section)],
-            store_sem.at[j],
-        )
-        copy.start()
-        return copy
+    stores = []
+
+    def late(k):
+        j, part = k // 2, k % 2
+        cut = section + (hours - section) // 16 * 8
+        first, rows = (section, cut - section) if part == 0 else (cut, hours - cut)
+        sweeps((j, 1), first, rows, lin, late_slope)
+        store = pltpu.make_async_copy(
+            d_v.at[j, pl.ds(first, rows)], out_d.at[j, pl.ds(first, rows)], store_sem.at[k]
+        )
+        store.start()
+        stores.append(store)
+
+    late_pieces = [functools.partial(late, k) for k in range(2 * scen)]
 
     def early(first):
         pieces = []
@@ -363,11 +386,9 @@
     copy.wait()
     pair1[0] = pair1[0] + part1[0]
     swap(0, chunks, d_hbm).start()
-    chain(0, d_hbm)
-    loads[1].wait()
-    loads[2].wait()
-    loads[3].wait()
-    stores = [late(0)]
+    for load in loads[1:]:
+        load.wait()
+    chain(0, d_hbm, late_pieces[:scen])
     for c in range(chunks + 1):
         back(0, c).wait_recv()
 
@@ -384,9 +405,9 @@
     dev_all[place] = spread_tile
     dev_copies = tiles(1, dev_all)
     late_stores = [
-        pltpu.make_async_copy(m_v, out_m, store_sem.at[scen]),
+        pltpu.make_async_copy(m_v, out_m, store_sem.at[2 * scen]),
         pltpu.make_async_copy(
-            d_v.at[:, pl.ds(0, section)], out_d.at[:, pl.ds(0, section)], store_sem.at[scen + 1]
+            d_v.at[:, pl.ds(0, section)], out_d.at[:, pl.ds(0, section)], store_sem.at[2 * scen + 1]
         ),
     ]
     for store in late_stores:
@@ -394,18 +415,16 @@
     copy.wait()
     pair1[1] = pair1[1] + part1[1]
     swap(1, chunks, d_v).start()
-    chain(1, d_v)
-    for j in range(1, scen):
-        stores.append(late(j))
+    chain(1, d_v, late_pieces[scen:])
     for c in range(chunks + 1):
         back(1, c).wait_recv()
     for j in range(scen):
         store = pltpu.make_async_copy(
-            avg1.at[1], out_a.at[j, pl.ds(0, DAY)], store_sem.at[scen + 2 + j]
+            avg1.at[1], out_a.at[j, pl.ds(0, DAY)], store_sem.at[2 * scen + 2 + j]
         )
         store.start()
         stores.append(store)
-    store = pltpu.make_async_copy(avg2.at[1], out_a.at[:, day2], store_sem.at[2 * scen + 2])
+    store = pltpu.make_async_copy(avg2.at[1], out_a.at[:, day2], store_sem.at[3 * scen + 2])
     store.start()
     stores.append(store)
     for copy in dev_copies:
@@ -467,8 +486,10 @@
             pltpu.VMEM((2, chunks, NODES_BR, DAY, LANES), f32),
             pltpu.VMEM((2, chunks, NODES_BR, DAY, LANES), f32),
             pltpu.VMEM((2, chunks, NODES_BR, DAY, LANES), f32),
+            pltpu.VMEM((2, chunks, NODES_BR, DAY, LANES), f32),
             pltpu.VMEM((2, chunks, scen, DAY, LANES), f32),
             pltpu.VMEM((2, scen, DAY, gens), f32),
+            pltpu.VMEM((2, DAY, gens // 2), f32),
             pltpu.VMEM((2, DAY, gens // 2), f32),
             pltpu.VMEM((2, DAY, gens // 2), f32),
             pltpu.VMEM((2, DAY, gens // 2), f32),
@@ -477,7 +498,7 @@
             pltpu.VMEM((2, DAY, gens), f32),
             pltpu.VMEM((2, DAY, gens), f32),
             dma((4,)),
-            dma((2 * scen + 3,)),
+            dma((3 * scen + 3,)),
             dma((2, 2 * n - 1)),
             dma((2, 2 * n - 1)),
             dma((2,)),

time: 205 us -> 128 us (0.62)
  Pallas kernels: 192 us -> 115 us
    pallas_call x1, Pallas kernels: 192 us -> 115 us  [shards(): pl.pallas_call(functools.partial(kernel, n, demand.shape[2]), out_shape=(...]
where the time goes in v3:
time: 128 us
  Pallas kernels  115 us (90%)
  local copies, waits for them, and re-layouts  12 us (9%)
    pallas_call x1, Pallas kernels, shards(): pl.pallas_call(functools.partial(kernel, n, demand.shape[2]), out_shape=(...  115 us
    unnamed x7, local copies, waits for them, and re-layouts  8.93 us

profile of v3, /device:TPU:0, one launch (start us, length us, event | category | flops | bytes accessed | tf_op | source)
XLA Modules:
  0.0 127.9 jit_solution(13715668724195513770)
XLA Ops:
  0.6 0.9 tile.4
  1.6 0.9 copy.15.dem_ref
  2.5 115.3 %shard_map.129 = (f32[4,168,2048]{2,1,0:T(8,128)}, f32[4,48,2048]{2,1,0:T(8,128)}, f32[4,48,2048]{2,1,0:T(8,128)}, f32[8,128]{1,0:T(8,128)}) custom-call(f32[4,168,2048]{2,1,0:T(8,128)} %d_hbm.1, f32[4,48,2048]{2,1,0:T(8,128)} %m_hbm.1, s32[4,168,2048]{2,1,0:T(8,128)} %com_hbm.1, f32[4,168,128]{2,1,0:T(8,128)} %copy.15.dem_ref, s32[1,2048]{1,0:T(1,128)} %bitcast.7, ...), custom_call_target="tpu_custom_call" | custom-call | tf_op jit(solution)/shard_map/pallas_call | solution.py:466
  117.8 1.2 slice.3
  119.0 0.0 copy-start.1
  119.0 5.8 %copy.19 = f32[4,168,2048]{2,1,0:T(8,128)} copy(f32[4,168,2048]{2,1,0:T(8,128)} %get-tuple-element.16) | data formatting | bytes 11010048
  124.8 0.0 copy-done.1
  124.8 0.0 copy-start
  124.8 1.1 copy.20
  126.0 0.8 copy-done
  126.8 1.1 copy.21
Async XLA Ops:
  119.0 5.8 %copy-start.1 = (f32[4,48,2048]{2,1,0:T(8,128)S(1)}, f32[4,48,2048]{2,1,0:T(8,128)}, u32[]{:S(2)}) copy-start(f32[4,48,2048]{2,1,0:T(8,128)} %get-tuple-element.17) | copy-start | bytes 4718596
  124.8 2.0 %copy-start = (f32[4,48,2048]{2,1,0:T(8,128)S(1)}, f32[4,48,2048]{2,1,0:T(8,128)}, u32[]{:S(2)}) copy-start(f32[4,48,2048]{2,1,0:T(8,128)} %get-tuple-element.18) | copy-start | bytes 4718596
